TPU v7x, 32 devices: a whole 2x2x4 slice. The times are simulated.
32 devices in a mesh: row: 4 (over z), col: 4 (over y, core), depth: 2 (over x).
Axes of the slice: x: 2, y: 2, z: 4, core: 2. Of those that a mesh axis runs over, the one named last changes fastest.
Arguments:
- tokens: bfloat16 [256, 12288], P(('row', 'col'), 'depth'), may hold values from -6 to 6
- in_weight: bfloat16 [12288, 49152], P('depth', ('row', 'col')), may hold values from -0.0546875 to 0.0546875
- in_bias: bfloat16 [49152], P(('row', 'col')), may hold values from -4 to 4
- out_weight: bfloat16 [49152, 12288], P(('row', 'col'), 'depth'), may hold values from -0.02734375 to 0.02734375
- out_bias: bfloat16 [12288], P('depth'), may hold values from -3 to 3
Outputs:
- outputs: bfloat16 [256, 12288], P(('row', 'col'), 'depth')
All inputs are finite; a program needn't handle non-finite values.
Results may differ from a plain program's by a relative error of at most 0.0045.
Values may be sent and summed in bfloat16 or wider, within the bound.
A program may use at most 192 MiB of HBM per device.

v0:
```python
import jax
import jax.numpy as jnp
from jax import lax
from jax.sharding import PartitionSpec as P


def body(tokens, in_weight, in_bias, out_weight, out_bias):
    partial_value = jnp.dot(
        lax.all_gather(tokens, ("row", "col"), axis=0, tiled=True),
        in_weight,
        preferred_element_type=jnp.float32,
    )
    bias_row = in_bias.astype(jnp.float32)
    summed = lax.psum(partial_value, "depth")
    hidden = jax.nn.gelu(summed + bias_row, approximate=True).astype(jnp.bfloat16)
    outputs = lax.psum_scatter(
        jnp.dot(hidden, out_weight, preferred_element_type=jnp.float32),
        ("row", "col"),
        scatter_dimension=0,
        tiled=True,
    )
    return (outputs + out_bias.astype(jnp.float32)).astype(jnp.bfloat16)


def solution(mesh):
    in_specs = (
        P(("row", "col"), "depth"),
        P("depth", ("row", "col")),
        P(("row", "col")),
        P(("row", "col"), "depth"),
        P("depth"),
    )
    out_specs = P(("row", "col"), "depth")
    return jax.shard_map(body, mesh=mesh, in_specs=in_specs, out_specs=out_specs, check_vma=False)
```

profile of v0, /device:TPU:0, one launch (start us, length us, event | category | flops | bytes accessed | tf_op | source)
XLA Modules:
  0.0 274.8 jit_solution(7004497836152599166)
XLA Ops:
  6.5 0.0 all-gather.2.cloned.1.call-start
  6.5 0.7 all-gather.2.cloned.1.call-update
  7.3 0.0 all-reduce.2.cloned.1.call-start
  7.3 50.3 %all-gather.2.cloned.1.call-done = bf16[256,6144]{1,0:T(8,128)(2,1)} async-done(((bf16[16,6144]{1,0:T(8,128)(2,1)}), bf16[256,6144]{1,0:T(8,128)(2,1)}) %all-gather.2.cloned.1.call-update) | async-done | bytes 3145744 | tf_op jit(solution)/shard_map/all_gather | solution.py:9
  57.6 18.8 %fusion.19 = f32[256,3072]{1,0:T(8,128)} fusion(bf16[256,6144]{1,0:T(8,128)(2,1)} %all-gather.2.cloned.1.call-done, bf16[6144,3072]{1,0:T(8,128)(2,1)} %param.6), kind=kOutput, calls=%fused_computation.20 | convolution fusion | flops 9663676416 | bytes 44040192 | tf_op jit(solution)/shard_map/dot_general | solution.py:8
  76.4 0.0 copy-start.1
  76.4 0.0 all-reduce.2.cloned.1.call-update
  76.4 0.0 reduce-scatter.2.cloned.1.call-start
  76.5 0.6 copy-done.1
  77.1 84.1 %all-reduce.2.cloned.1.call-done = f32[256,3072]{1,0:T(8,128)} async-done(((f32[256,3072]{1,0:T(8,128)}), f32[256,3072]{1,0:T(8,128)}) %all-reduce.2.cloned.1.call-update) | async-done | bytes 3145744 | tf_op jit(solution)/shard_map/psum | solution.py:14
  161.1 19.9 %fusion.8 = f32[256,6144]{1,0:T(8,128)} fusion(bf16[3072,6144]{1,0:T(8,128)(2,1)} %param.8, f32[256,3072]{1,0:T(8,128)} %all-reduce.2.cloned.1.call-done, f32[3072]{0:T(1024)S(1)} %convert_element_type.12), kind=kOutput, calls=%fused_computation.9 | convolution fusion | flops 9671540736 | bytes 47198208 | tf_op jit(solution)/shard_map/dot_general | solution.py:17
  181.1 0.0 copy-start
  181.1 0.0 reduce-scatter.2.cloned.1.call-update
  181.1 0.7 copy-done
  181.8 84.7 %reduce-scatter.2.cloned.1.call-done = f32[16,6144]{1,0:T(8,128)} async-done(((f32[256,6144]{1,0:T(8,128)}), f32[16,6144]{1,0:T(8,128)}) %reduce-scatter.2.cloned.1.call-update) | async-done | bytes 393232 | tf_op jit(solution)/shard_map/reduce_scatter | solution.py:16
  266.5 1.7 add_convert_fusion
  (2 shorter events, 0.0 us)
Async XLA Ops:
  6.5 51.0 %all-gather.2.cloned.1.call-start = ((), (), s32[]{:S(2)}) async-start(), calls=%async_computation.1 | async-start | bytes 3342336 | tf_op jit(solution)/shard_map/all_gather | solution.py:9
  7.3 153.9 %all-reduce.2.cloned.1.call-start = ((), (), s32[]{:S(2)}) async-start(), calls=%async_computation.2 | async-start | bytes 6291456 | tf_op jit(solution)/shard_map/psum | solution.py:14
  76.4 0.7 copy-start.1
  76.4 190.1 %reduce-scatter.2.cloned.1.call-start = ((), (), s32[]{:S(2)}) async-start(), calls=%async_computation.3 | async-start | bytes 6684672 | tf_op jit(solution)/shard_map/reduce_scatter | solution.py:16
  181.1 0.7 copy-start
Sparse Core Ops, SparseCore 0:
  9.6 47.8 all-gather.1
  76.5 84.5 all-reduce.1
  181.2 85.2 reduce-scatter.1
where the time goes:
time: 275 us
  waiting for transfers between devices  220 us (80%)
  matrix products  38.8 us (14%)
  between operations  13.1 us (5%)
    reduce_scatter x1, waiting for transfers between devices, body(): lax.psum_scatter(jnp.dot(hidden, out_weight, preferred_element_type=jnp.f...  84.7 us
    psum x1, waiting for transfers between devices, body(): summed = lax.psum(partial_value, 'depth')  84.1 us
    all_gather x1, waiting for transfers between devices, body(): lax.all_gather(tokens, ('row', 'col'), axis=0, tiled=True)  50.3 us
    dot_general x1, matrix products, body(): jnp.dot(hidden, out_weight, preferred_element_type=jnp.float32)  19.9 us
    dot_general x1, matrix products, body(): jnp.dot(lax.all_gather(tokens, ('row', 'col'), axis=0, tiled=True), in_we...  18.8 us
  transfers between devices with their start and end apart: 3, of which 3 were waited for; matrix products, arithmetic and copies ran while one was open for 0% of the time, Pallas kernels for 0%

commit v1 on v0

v1 whole, which is shorter than its diff:
```python
import functools

import jax
import jax.numpy as jnp
from jax import lax
from jax.experimental import pallas as pl
from jax.experimental.pallas import tpu as pltpu
from jax.sharding import PartitionSpec as P

CORES = 2
BF16 = jnp.bfloat16
F32 = jnp.float32


def kernel(
    R, C, DP, tps, nch, nb, ch,
    x_ref, w1_ref, b1_ref, w2_ref, b2_ref, out_ref,
    xbuf, slots, own, psend, precv, hbuf, acc, s1s, s1r, s2s, s2r, own2, s3s, s3r,
    w1_sem, w2_sem, ag_ss, ag_rs, p_ss, p_rs, s1_ss, s1_rs, s2_ss, s2_rs, s3_ss, s3_rs,
):
    Y = C // CORES
    z = lax.axis_index("row")
    col = lax.axis_index("col")
    dp = lax.axis_index("depth")
    y = col // CORES
    c = col % CORES
    sib = y * CORES + (1 - c)

    def remote(src, dst, ss, rs, **dev):
        return pltpu.make_async_remote_copy(
            src_ref=src, dst_ref=dst, send_sem=ss, recv_sem=rs,
            device_id=dev, device_id_type=pl.DeviceIdType.MESH,
        )

    def w1_copy(k):
        return pltpu.make_async_copy(w1_ref.at[:, pl.ds(pl.multiple_of(k * ch, ch), ch)], slots.at[k], w1_sem.at[k])

    def w2_copy(k, n):
        return pltpu.make_async_copy(
            w2_ref.at[pl.ds(pl.multiple_of(k * ch, ch), ch), pl.ds(pl.multiple_of(n * ch, ch), ch)],
            slots.at[k, pl.ds(pl.multiple_of(n * ch, ch), ch)],
            w2_sem.at[k, n],
        )

    @pl.loop(0, nch)
    def _(k):
        w1_copy(k).start()

    barrier = pltpu.get_barrier_semaphore()

    def greet(**dev):
        pl.semaphore_signal(barrier, inc=1, device_id=dev, device_id_type=pl.DeviceIdType.MESH)

    z_peers = [(z + dz) % R for dz in range(1, R)]
    y_peers = [(y + dy) % Y for dy in range(1, Y)]
    d_peers = [(dp + dd) % DP for dd in range(1, DP)]
    for zt in z_peers:
        greet(row=zt)
    for yt in y_peers:
        greet(col=yt * CORES + c)
    greet(col=sib)
    for dt in d_peers:
        greet(depth=dt)

    def shard(zz, yy, cc):
        return zz * C + yy * CORES + cc

    def rows(s):
        return pl.ds(pl.multiple_of(s * tps, tps), tps)

    me = shard(z, y, c)
    xbuf[rows(me)] = x_ref[...]
    pl.semaphore_wait(barrier, (R - 1) + (Y - 1) + 1 + (DP - 1))

    sent = []

    def send_shard(s, **dev):
        copy = remote(xbuf.at[rows(s)], xbuf.at[rows(s)], ag_ss.at[len(sent)], ag_rs.at[s], **dev)
        copy.start()
        sent.append(copy)

    def await_shard(s):
        remote(xbuf.at[rows(s)], xbuf.at[rows(s)], ag_ss.at[0], ag_rs.at[s], col=sib).wait_recv()

    for zt in z_peers:
        send_shard(me, row=zt)
    for yt in y_peers:
        send_shard(me, col=yt * CORES + c)
    send_shard(me, col=sib)

    @pl.loop(0, nb)
    def _(n):
        acc[n] = jnp.zeros(acc.shape[1:], F32)

    for zt in z_peers:
        s = shard(zt, y, c)
        await_shard(s)
        for yt in y_peers:
            send_shard(s, col=yt * CORES + c)
        send_shard(s, col=sib)
    for yt in y_peers:
        for zt in [z] + z_peers:
            s = shard(zt, yt, c)
            await_shard(s)
            send_shard(s, col=sib)
    for yt in [y] + y_peers:
        for zt in [z] + z_peers:
            await_shard(shard(zt, yt, 1 - c))

    def p_copy(i, k):
        return remote(psend.at[k], precv.at[i, k], p_ss.at[i, k], p_rs.at[i, k], depth=d_peers[i])

    @pl.loop(0, nch)
    def _(k):
        w1_copy(k).wait()
        partial = jnp.dot(xbuf[...], slots[k], preferred_element_type=F32)
        own[k] = partial
        psend[k] = partial.astype(BF16)
        for i in range(DP - 1):
            p_copy(i, k).start()

        @pl.loop(0, nb)
        def _(n):
            w2_copy(k, n).start()

    def hidden(k):
        for i in range(DP - 1):
            p_copy(i, k).wait_recv()
        pre = own[k]
        for i in range(DP - 1):
            pre = pre + precv[i, k].astype(F32)
        pre = pre + b1_ref[:, pl.ds(pl.multiple_of(k * ch, ch), ch)].astype(F32)
        hbuf[...] = jax.nn.gelu(pre, approximate=True).astype(BF16)

    def accumulate(k, n):
        w2_copy(k, n).wait()
        acc[n] += jnp.dot(
            hbuf[...], slots[k, pl.ds(pl.multiple_of(n * ch, ch), ch)], preferred_element_type=F32
        )

    @pl.loop(0, nch - 1)
    def _(k):
        hidden(k)

        @pl.loop(0, nb)
        def _(n):
            accumulate(k, n)

    def s1_copy(n):
        return remote(s1s.at[n], s1r.at[n], s1_ss.at[n], s1_rs.at[n], col=sib)

    def s2_copy(i, n):
        return remote(s2s.at[i, n], s2r.at[i, n], s2_ss.at[i, n], s2_rs.at[i, n], col=y_peers[i] * CORES + c)

    def s3_copy(i, n):
        return remote(s3s.at[i, n], s3r.at[i, n], s3_ss.at[i, n], s3_rs.at[i, n], row=z_peers[i])

    def stage2(n):
        s1_copy(n).wait_recv()

        def chip_sum(j):
            return acc[n, rows(CORES * j + c)] + s1r[n, rows(j)].astype(F32)

        for i, yt in enumerate(y_peers):
            for zz in range(R):
                s2s[i, n, rows(zz)] = chip_sum(zz * Y + yt).astype(BF16)
            s2_copy(i, n).start()
        for zz in range(R):
            own2[n, rows(zz)] = chip_sum(zz * Y + y)

    hidden(nch - 1)

    @pl.loop(0, nb)
    def _(n):
        accumulate(nch - 1, n)
        for j in range(R * Y):
            s1s[n, rows(j)] = acc[n, rows(CORES * j + 1 - c)].astype(BF16)
        s1_copy(n).start()

        @pl.when(n > 0)
        def _():
            stage2(n - 1)

    stage2(nb - 1)

    @pl.loop(0, nb)
    def _(n):
        total = own2[n]
        for i in range(Y - 1):
            s2_copy(i, n).wait_recv()
        for i in range(Y - 1):
            total = total + s2r[i, n].astype(F32)
        own2[n] = total
        for i, zt in enumerate(z_peers):
            s3s[i, n] = own2[n, rows(zt)].astype(BF16)
            s3_copy(i, n).start()

    @pl.loop(0, nb)
    def _(n):
        cols = pl.ds(pl.multiple_of(n * ch, ch), ch)
        for i in range(R - 1):
            s3_copy(i, n).wait_recv()
        total = own2[n, rows(z)]
        for i in range(R - 1):
            total = total + s3r[i, n].astype(F32)
        out_ref[:, cols] = (total + b2_ref[:, cols].astype(F32)).astype(BF16)

    for copy in sent:
        copy.wait_send()

    @pl.loop(0, nch)
    def _(k):
        for i in range(DP - 1):
            p_copy(i, k).wait_send()

    @pl.loop(0, nb)
    def _(n):
        s1_copy(n).wait_send()
        for i in range(Y - 1):
            s2_copy(i, n).wait_send()
        for i in range(R - 1):
            s3_copy(i, n).wait_send()


def solution(mesh):
    R, C, DP = mesh.shape["row"], mesh.shape["col"], mesh.shape["depth"]
    Y = C // CORES

    def body(tokens, in_weight, in_bias, out_weight, out_bias):
        tps, dl = tokens.shape
        ffl = in_weight.shape[1]
        T = tps * R * C
        ch = 512
        nch, nb = ffl // ch, dl // ch
        n_ag = (R - 1) + (Y - 1) + 1 + (R - 1) * Y + (Y - 1) * R
        vmem = pl.BlockSpec(memory_space=pltpu.VMEM)
        hbm = pl.BlockSpec(memory_space=pl.ANY)
        dma = pltpu.SemaphoreType.DMA
        return pl.pallas_call(
            functools.partial(kernel, R, C, DP, tps, nch, nb, ch),
            out_shape=jax.ShapeDtypeStruct((tps, dl), BF16),
            in_specs=[vmem, hbm, vmem, hbm, vmem],
            out_specs=vmem,
            scratch_shapes=[
                pltpu.VMEM((T, dl), BF16),
                pltpu.VMEM((nch, dl, ch), BF16),
                pltpu.VMEM((nch, T, ch), F32),
                pltpu.VMEM((nch, T, ch), BF16),
                pltpu.VMEM((DP - 1, nch, T, ch), BF16),
                pltpu.VMEM((T, ch), BF16),
                pltpu.VMEM((nb, T, ch), F32),
                pltpu.VMEM((nb, T // CORES, ch), BF16),
                pltpu.VMEM((nb, T // CORES, ch), BF16),
                pltpu.VMEM((Y - 1, nb, R * tps, ch), BF16),
                pltpu.VMEM((Y - 1, nb, R * tps, ch), BF16),
                pltpu.VMEM((nb, R * tps, ch), F32),
                pltpu.VMEM((R - 1, nb, tps, ch), BF16),
                pltpu.VMEM((R - 1, nb, tps, ch), BF16),
                dma((nch,)),
                dma((nch, nb)),
                dma((n_ag,)),
                dma((R * C,)),
                dma((DP - 1, nch)),
                dma((DP - 1, nch)),
                dma((nb,)),
                dma((nb,)),
                dma((Y - 1, nb)),
                dma((Y - 1, nb)),
                dma((R - 1, nb)),
                dma((R - 1, nb)),
            ],
            compiler_params=pltpu.CompilerParams(
                collective_id=0, has_side_effects=True, vmem_limit_bytes=63 * 1024 * 1024
            ),
        )(tokens, in_weight, in_bias.reshape(1, ffl), out_weight, out_bias.reshape(1, dl))

    in_specs = (
        P(("row", "col"), "depth"),
        P("depth", ("row", "col")),
        P(("row", "col")),
        P(("row", "col"), "depth"),
        P("depth"),
    )
    out_specs = P(("row", "col"), "depth")
    return jax.shard_map(body, mesh=mesh, in_specs=in_specs, out_specs=out_specs, check_vma=False)
```

time: 275 us -> 108 us (0.39)
  waiting for transfers between devices: 220 us -> 0 us
  Pallas kernels: 0 us -> 103 us
  matrix products: 38.8 us -> 0 us
  between operations: 13.1 us -> 0.01 us
  local copies, waits for them, and re-layouts: 1.3 us -> 4.24 us
    pallas_call x0 -> x1, Pallas kernels: none -> 103 us  [body(): pl.pallas_call(functools.partial(kernel, R, C, DP, tps, nch, nb, ch), out...]
    reduce_scatter x1 -> x0, waiting for transfers between devices: 84.7 us -> none  [body(): lax.psum_scatter(jnp.dot(hidden, out_weight, preferred_element_type=jnp.f...]
    psum x1 -> x0, waiting for transfers between devices: 84.1 us -> none  [body(): summed = lax.psum(partial_value, 'depth')]
    all_gather x1 -> x0, waiting for transfers between devices: 50.3 us -> none  [body(): lax.all_gather(tokens, ('row', 'col'), axis=0, tiled=True)]
    dot_general x2 -> x0, matrix products: 38.8 us -> none  [the longest x1 19.9 us: body(): jnp.dot(hidden, out_weight, preferred_element_type=jnp.float32)]
  transfers between devices with their start and end apart: 3 -> 0, of which waited for: 3 -> 0; matrix products, arithmetic and copies ran while one was open for 0% -> 0% of each run, Pallas kernels for 0% -> 0%
where the time goes in v1:
time: 108 us
  Pallas kernels  103 us (95%)
  local copies, waits for them, and re-layouts  4.24 us (4%)
    pallas_call x1, Pallas kernels, body(): pl.pallas_call(functools.partial(kernel, R, C, DP, tps, nch, nb, ch), out...  103 us

profile of v1, /device:TPU:0, one launch (start us, length us, event | category | flops | bytes accessed | tf_op | source)
XLA Modules:
  0.0 107.6 jit_solution(12251746484200132620)
XLA Ops:
  0.0 1.3 %reshape.6.b1_ref = bf16[1,3072]{1,0:T(2,128)(2,1)} reshape(bf16[3072]{0:T(1024)(128)(2,1)} %param.7) | data formatting | bytes 12288 | tf_op jit(solution)/shard_map/reshape | solution.py:275
  1.3 1.3 %reshape.7.b2_ref = bf16[1,6144]{1,0:T(2,128)(2,1)} reshape(bf16[6144]{0:T(1024)(128)(2,1)} %param.9) | data formatting | bytes 24576 | tf_op jit(solution)/shard_map/reshape | solution.py:275
  2.6 103.3 %shard_map.55 = bf16[16,6144]{1,0:T(8,128)(2,1)} custom-call(bf16[16,6144]{1,0:T(8,128)(2,1)} %x_ref.1, bf16[6144,3072]{1,0:T(8,128)(2,1)} %w1_ref.1, bf16[1,3072]{1,0:T(2,128)(2,1)} %reshape.6.b1_ref, bf16[3072,6144]{1,0:T(8,128)(2,1)} %w2_ref.1, bf16[1,6144]{1,0:T(2,128)(2,1)} %reshape.7.b2_ref), custom_call_target="tpu_custom_call" | custom-call | tf_op jit(solution)/shard_map/pallas_call | solution.py:239
  105.9 1.6 %copy.7 = bf16[16,6144]{1,0:T(8,128)(2,1)} copy(bf16[16,6144]{1,0:T(8,128)(2,1)} %shard_map.55) | data formatting | bytes 393216

commit v2 on v1

--- a/solution.py
+++ b/solution.py
@@ -10,6 +10,17 @@
 CORES = 2
 BF16 = jnp.bfloat16
 F32 = jnp.float32
+
+
+def partner(i, step, n):
+    if n & (n - 1):
+        return (i + step) % n
+    out, bit = 0, 1
+    while bit < n:
+        own = i // bit % 2
+        out = out + bit * (1 - own if step & bit else own)
+        bit *= 2
+    return out
 
 
 def kernel(
@@ -35,11 +46,15 @@
     def w1_copy(k):
         return pltpu.make_async_copy(w1_ref.at[:, pl.ds(pl.multiple_of(k * ch, ch), ch)], slots.at[k], w1_sem.at[k])
 
-    def w2_copy(k, n):
+    ffl = w2_ref.shape[0]
+    per = nb // nch
+
+    def w2_slot(n):
+        return n // per, pl.ds(pl.multiple_of(n % per * ffl, ffl), ffl)
+
+    def w2_copy(n):
         return pltpu.make_async_copy(
-            w2_ref.at[pl.ds(pl.multiple_of(k * ch, ch), ch), pl.ds(pl.multiple_of(n * ch, ch), ch)],
-            slots.at[k, pl.ds(pl.multiple_of(n * ch, ch), ch)],
-            w2_sem.at[k, n],
+            w2_ref.at[:, pl.ds(pl.multiple_of(n * ch, ch), ch)], slots.at[w2_slot(n)], w2_sem.at[n]
         )
 
     @pl.loop(0, nch)
@@ -51,7 +66,15 @@
     def greet(**dev):
         pl.semaphore_signal(barrier, inc=1, device_id=dev, device_id_type=pl.DeviceIdType.MESH)
 
-    z_peers = [(z + dz) % R for dz in range(1, R)]
+    z_peers = [partner(z, dz, R) for dz in range(1, R)]
+    chain = R == 4
+    far = 1 - z // (R // 2)
+    if chain:
+        z_order = [z, partner(z, 1, R), 1 + far, 3 * far]
+        across = 3 - z
+        inner = (z == 1) | (z == 2)
+    else:
+        z_order = [z] + z_peers
     y_peers = [(y + dy) % Y for dy in range(1, Y)]
     d_peers = [(dp + dd) % DP for dd in range(1, DP)]
     for zt in z_peers:
@@ -74,77 +97,109 @@
 
     sent = []
 
-    def send_shard(s, **dev):
+    def send_shard(s, inner_only=False, **dev):
         copy = remote(xbuf.at[rows(s)], xbuf.at[rows(s)], ag_ss.at[len(sent)], ag_rs.at[s], **dev)
-        copy.start()
-        sent.append(copy)
+        sent.append((copy, inner_only))
+        if inner_only:
+            pl.when(inner)(copy.start)
+        else:
+            copy.start()
 
     def await_shard(s):
         remote(xbuf.at[rows(s)], xbuf.at[rows(s)], ag_ss.at[0], ag_rs.at[s], col=sib).wait_recv()
 
-    for zt in z_peers:
-        send_shard(me, row=zt)
+    if chain:
+        send_shard(me, inner_only=True, row=across)
+        send_shard(me, row=z_order[1])
+    else:
+        for zt in z_peers:
+            send_shard(me, row=zt)
     for yt in y_peers:
         send_shard(me, col=yt * CORES + c)
     send_shard(me, col=sib)
 
-    @pl.loop(0, nb)
-    def _(n):
-        acc[n] = jnp.zeros(acc.shape[1:], F32)
-
-    for zt in z_peers:
-        s = shard(zt, y, c)
+    def forward_z(i):
+        s = shard(z_order[i], y, c)
         await_shard(s)
+        if chain:
+            send_shard(s, inner_only=True, row=across if i == 1 else z_order[1])
         for yt in y_peers:
             send_shard(s, col=yt * CORES + c)
         send_shard(s, col=sib)
-    for yt in y_peers:
-        for zt in [z] + z_peers:
-            s = shard(zt, yt, c)
+
+    def forward_y(i):
+        for yt in y_peers:
+            s = shard(z_order[i], yt, c)
             await_shard(s)
             send_shard(s, col=sib)
-    for yt in [y] + y_peers:
-        for zt in [z] + z_peers:
-            await_shard(shard(zt, yt, 1 - c))
-
-    def p_copy(i, k):
-        return remote(psend.at[k], precv.at[i, k], p_ss.at[i, k], p_rs.at[i, k], depth=d_peers[i])
-
-    @pl.loop(0, nch)
-    def _(k):
-        w1_copy(k).wait()
-        partial = jnp.dot(xbuf[...], slots[k], preferred_element_type=F32)
-        own[k] = partial
-        psend[k] = partial.astype(BF16)
-        for i in range(DP - 1):
-            p_copy(i, k).start()
-
-        @pl.loop(0, nb)
-        def _(n):
-            w2_copy(k, n).start()
+
+    half = R // 2
+
+    def block_rows(b):
+        size = half * C * tps
+        return pl.ds(pl.multiple_of((1 - far if b == 0 else far) * size, size), size)
+
+    def p_copy(i, k, b):
+        r = block_rows(b)
+        return remote(
+            psend.at[k, r], precv.at[i, k, r], p_ss.at[i, k, b], p_rs.at[i, k, b], depth=d_peers[i]
+        )
+
+    def project(b, first, last):
+        r = block_rows(b)
+
+        @pl.loop(first, last)
+        def _(k):
+            if b == 0:
+                w1_copy(k).wait()
+            partial = jnp.dot(xbuf[r], slots[k], preferred_element_type=F32)
+            own[k, r] = partial
+            psend[k, r] = partial.astype(BF16)
+            for i in range(DP - 1):
+                p_copy(i, k, b).start()
+            if b == 1:
+                for j in range(per):
+                    w2_copy(k * per + j).start()
+
+    def await_block(b):
+        for i in range(b * half, (b + 1) * half):
+            for yt in [y] + y_peers:
+                await_shard(shard(z_order[i], yt, 1 - c))
+
+    for i in range(1, half):
+        forward_z(i)
+    for i in range(half):
+        forward_y(i)
+    forward_z(half)
+    await_block(0)
+    cut1, cut2 = nch // 3, 2 * nch // 3
+    project(0, 0, cut1)
+    for i in range(half + 1, R):
+        forward_z(i)
+    forward_y(half)
+    project(0, cut1, cut2)
+    for i in range(half + 1, R):
+        forward_y(i)
+    project(0, cut2, nch)
+    await_block(1)
+    project(1, 0, nch)
 
     def hidden(k):
         for i in range(DP - 1):
-            p_copy(i, k).wait_recv()
+            for b in range(2):
+                p_copy(i, k, b).wait_recv()
         pre = own[k]
         for i in range(DP - 1):
             pre = pre + precv[i, k].astype(F32)
-        pre = pre + b1_ref[:, pl.ds(pl.multiple_of(k * ch, ch), ch)].astype(F32)
-        hbuf[...] = jax.nn.gelu(pre, approximate=True).astype(BF16)
-
-    def accumulate(k, n):
-        w2_copy(k, n).wait()
-        acc[n] += jnp.dot(
-            hbuf[...], slots[k, pl.ds(pl.multiple_of(n * ch, ch), ch)], preferred_element_type=F32
-        )
-
-    @pl.loop(0, nch - 1)
-    def _(k):
-        hidden(k)
-
-        @pl.loop(0, nb)
-        def _(n):
-            accumulate(k, n)
+        cols = pl.ds(pl.multiple_of(k * ch, ch), ch)
+        pre = pre + b1_ref[:, cols].astype(F32)
+        hbuf[:, cols] = jax.nn.gelu(pre, approximate=True).astype(BF16)
+
+    def multiply(n):
+        w2_copy(n).wait()
+        acc[n] = jnp.dot(hbuf[...], slots[w2_slot(n)], preferred_element_type=F32)
+
+    pl.loop(0, nch)(hidden)
 
     def s1_copy(n):
         return remote(s1s.at[n], s1r.at[n], s1_ss.at[n], s1_rs.at[n], col=sib)
@@ -168,11 +223,9 @@
         for zz in range(R):
             own2[n, rows(zz)] = chip_sum(zz * Y + y)
 
-    hidden(nch - 1)
-
     @pl.loop(0, nb)
     def _(n):
-        accumulate(nch - 1, n)
+        multiply(n)
         for j in range(R * Y):
             s1s[n, rows(j)] = acc[n, rows(CORES * j + 1 - c)].astype(BF16)
         s1_copy(n).start()
@@ -205,13 +258,17 @@
             total = total + s3r[i, n].astype(F32)
         out_ref[:, cols] = (total + b2_ref[:, cols].astype(F32)).astype(BF16)
 
-    for copy in sent:
-        copy.wait_send()
+    for copy, inner_only in sent:
+        if inner_only:
+            pl.when(inner)(copy.wait_send)
+        else:
+            copy.wait_send()
 
     @pl.loop(0, nch)
     def _(k):
         for i in range(DP - 1):
-            p_copy(i, k).wait_send()
+            for b in range(2):
+                p_copy(i, k, b).wait_send()
 
     @pl.loop(0, nb)
     def _(n):
@@ -232,7 +289,7 @@
         T = tps * R * C
         ch = 512
         nch, nb = ffl // ch, dl // ch
-        n_ag = (R - 1) + (Y - 1) + 1 + (R - 1) * Y + (Y - 1) * R
+        n_ag = 3 * R * Y + R
         vmem = pl.BlockSpec(memory_space=pltpu.VMEM)
         hbm = pl.BlockSpec(memory_space=pl.ANY)
         dma = pltpu.SemaphoreType.DMA
@@ -247,7 +304,7 @@
                 pltpu.VMEM((nch, T, ch), F32),
                 pltpu.VMEM((nch, T, ch), BF16),
                 pltpu.VMEM((DP - 1, nch, T, ch), BF16),
-                pltpu.VMEM((T, ch), BF16),
+                pltpu.VMEM((T, ffl), BF16),
                 pltpu.VMEM((nb, T, ch), F32),
                 pltpu.VMEM((nb, T // CORES, ch), BF16),
                 pltpu.VMEM((nb, T // CORES, ch), BF16),
@@ -257,11 +314,11 @@
                 pltpu.VMEM((R - 1, nb, tps, ch), BF16),
                 pltpu.VMEM((R - 1, nb, tps, ch), BF16),
                 dma((nch,)),
-                dma((nch, nb)),
+                dma((nb,)),
                 dma((n_ag,)),
                 dma((R * C,)),
-                dma((DP - 1, nch)),
-                dma((DP - 1, nch)),
+                dma((DP - 1, nch, 2)),
+                dma((DP - 1, nch, 2)),
                 dma((nb,)),
                 dma((nb,)),
                 dma((Y - 1, nb)),

time: 108 us -> 94.7 us (0.88)
  Pallas kernels: 103 us -> 90.2 us
    pallas_call x1, Pallas kernels: 103 us -> 90.2 us  [body(): pl.pallas_call(functools.partial(kernel, R, C, DP, tps, nch, nb, ch), out...]
where the time goes in v2:
time: 94.7 us; the launch traced here: 94.5 us
  Pallas kernels  90.2 us (95%)
  local copies, waits for them, and re-layouts  4.24 us (4%)
    pallas_call x1, Pallas kernels, body(): pl.pallas_call(functools.partial(kernel, R, C, DP, tps, nch, nb, ch), out...  90.2 us

profile of v2, /device:TPU:0, one launch (start us, length us, event | category | flops | bytes accessed | tf_op | source)
XLA Modules:
  0.0 94.5 jit_solution(8598234389199131153)
XLA Ops:
  0.0 1.3 %reshape.6.b1_ref = bf16[1,3072]{1,0:T(2,128)(2,1)} reshape(bf16[3072]{0:T(1024)(128)(2,1)} %param.7) | data formatting | bytes 12288 | tf_op jit(solution)/shard_map/reshape | solution.py:332
  1.3 1.3 %reshape.7.b2_ref = bf16[1,6144]{1,0:T(2,128)(2,1)} reshape(bf16[6144]{0:T(1024)(128)(2,1)} %param.9) | data formatting | bytes 24576 | tf_op jit(solution)/shard_map/reshape | solution.py:332
  2.6 90.2 %shard_map.55 = bf16[16,6144]{1,0:T(8,128)(2,1)} custom-call(bf16[16,6144]{1,0:T(8,128)(2,1)} %x_ref.1, bf16[6144,3072]{1,0:T(8,128)(2,1)} %w1_ref.1, bf16[1,3072]{1,0:T(2,128)(2,1)} %reshape.6.b1_ref, bf16[3072,6144]{1,0:T(8,128)(2,1)} %w2_ref.1, bf16[1,6144]{1,0:T(2,128)(2,1)} %reshape.7.b2_ref), custom_call_target="tpu_custom_call" | custom-call | tf_op jit(solution)/shard_map/pallas_call | solution.py:296
  92.8 1.6 %copy.7 = bf16[16,6144]{1,0:T(8,128)(2,1)} copy(bf16[16,6144]{1,0:T(8,128)(2,1)} %shard_map.55) | data formatting | bytes 393216
